TPU v7x, 32 devices: a whole 2x2x4 slice. The times are simulated.
32 devices in a mesh: sub: 8 (over z, x), panel: 4 (over y, core).
Axes of the slice: x: 2, y: 2, z: 4, core: 2. Of those that a mesh axis runs over, the one named last changes fastest.
Arguments:
- border_factor: bfloat16 [8, 1024, 4096], P('sub', None, 'panel'), may hold values from -0.119628906 to 0.119628906
- tile_mask: int32 [8, 8, 32], P('sub', None, 'panel'), may hold values 0 or 1
- front_maps: int32 [3, 8, 1024], replicated, may hold values from 0 to 1279, as said below
- sep_inverse: float32 [3, 256, 256], replicated, may hold values from -1 to 5, as said below
- sep_scale: float32 [3, 8, 256], replicated, may hold values from 0.25 to 1.75
Outputs:
- border_schur: float32 [8, 1024, 1024], P('sub', 'panel')
Inputs may be any that keep to these rules, and one draw needn't show every extreme that they name: `front_maps`: entry [l, c, i] lies in front block i // 256, that is from (i // 256) * 320 to (i // 256) * 320 + 319, and the 256 entries of one child in one block are distinct. `sep_inverse`: each level's matrix is symmetric.
All inputs are finite; a program needn't handle non-finite values. No bound on the sum of `tile_mask` on one device may be relied on, other than what follows from the above.
Results may differ from a plain program's by a relative error of at most 0.0003.
Values sent between devices are 32-bit elements; how exact they have to be, the bound alone decides.
A program may use at most 64 MiB of HBM per device.

v0:
```python
import functools

import jax
import jax.numpy as jnp
from jax import lax
from jax.experimental import pallas as pl
from jax.experimental.pallas import tpu as pltpu
from jax.sharding import PartitionSpec as P

BORDER = 1024
SEP = 256
TILE = 128
LEVELS = 3
CORES = 2
QUARTERS = 4
F32 = jnp.float32
BF16 = jnp.bfloat16


def nn(a, b):
    return lax.dot_general(a, b, (((1,), (0,)), ((), ())), preferred_element_type=F32)


def nt(a, b):
    return lax.dot_general(a, b, (((1,), (1,)), ((), ())), preferred_element_type=F32)


def split(x):
    high = x.astype(BF16)
    return high, (x - high.astype(F32)).astype(BF16)


def product(a, b):
    a_high, a_low = split(a)
    b_high, b_low = split(b)
    return nn(a_high, b_high) + nn(a_high, b_low) + nn(a_low, b_high)


def kernel(
    panels,
    mask_ref,
    factor_ref,
    maps_ref,
    inverse_ref,
    scale_ref,
    out_ref,
    masked,
    a_send,
    a_recv,
    own,
    b_send,
    b_recv,
    c_send,
    c_recv,
    w0,
    w1,
    w2,
    v0,
    v1,
    v2,
    bb0,
    d_send,
    d_recv,
    e_send,
    e_recv,
    fin,
    send_sem,
    recv_sem,
):
    chips = panels // CORES
    brows = BORDER // panels
    srows = SEP // panels
    fronts = brows + srows
    quarter = BORDER // QUARTERS
    qsep = SEP // QUARTERS
    p = lax.axis_index("panel")
    s = lax.axis_index("sub")
    y, core = p // CORES, p % CORES
    bit0, bit1, bit2 = s % 2, s // 2 % 2, s // 4 % 2
    base = s - s % 8
    sub1 = base + bit2 * 4 + bit1 * 2 + (1 - bit0)
    sub2 = base + bit2 * 4 + (1 - bit1) * 2 + bit0
    sub3 = base + bit2 * 4 + (1 - bit1) * 2 + (1 - bit0)
    sub4 = base + (1 - bit2) * 4 + bit1 * 2 + bit0
    partner = y * CORES + 1 - core
    others = [(y + d) % chips for d in range(1, chips)]

    barrier = pltpu.get_barrier_semaphore()
    greeted = [{"panel": partner}] + [
        {"panel": other * CORES + core} for other in others
    ] + [{"sub": sub} for sub in (sub1, sub2, sub3, sub4)]
    for device in greeted:
        pl.semaphore_signal(barrier, inc=1, device_id=device, device_id_type=pl.DeviceIdType.MESH)

    started = []

    def send(src, dst, device):
        at = len(started)
        copy = pltpu.make_async_remote_copy(
            src_ref=src,
            dst_ref=dst,
            send_sem=send_sem.at[at],
            recv_sem=recv_sem.at[at],
            device_id=device,
            device_id_type=pl.DeviceIdType.MESH,
        )
        copy.start()
        started.append(copy)
        return copy

    for i in range(mask_ref.shape[1]):
        for j in range(mask_ref.shape[2]):
            keep = jnp.full((TILE, TILE), mask_ref[0, i, j].astype(F32), F32).astype(BF16)
            rows, cols = pl.ds(i * TILE, TILE), pl.ds(j * TILE, TILE)
            masked[rows, cols] = factor_ref[0, rows, cols] * keep

    def rows_of(chip, core_there):
        start = pl.multiple_of((chip * CORES + core_there) * brows, brows)
        return masked[pl.ds(start, brows), :]

    first = 2 * (1 - bit0)
    second = 2 * bit0
    order = (first, first + 1, second, second + 1)
    a_copies, b_copies = [], []

    def forward(k):
        a_copies[k].wait_recv()
        copies = []
        for d, other in enumerate(others):
            b_send[k, d] = own[k, other] + a_recv[k, other]
            copies.append(send(b_send.at[k, d], b_recv.at[k, d], {"panel": other * CORES + core}))
        b_copies.append(copies)

    for k, q in enumerate(order):
        columns = masked[pl.ds(pl.multiple_of(q * quarter, quarter), quarter), :]
        for chip in range(chips):
            a_send[k, chip] = nt(rows_of(chip, 1 - core), columns)
        if k == 0:
            pl.semaphore_wait(barrier, len(greeted))
        a_copies.append(send(a_send.at[k], a_recv.at[k], {"panel": partner}))
        for chip in range(chips):
            own[k, chip] = nt(rows_of(chip, core), columns)
        if k:
            forward(k - 1)
    forward(len(order) - 1)

    def map_of(level, child, start, size):
        rows = maps_ref[level, :, pl.ds(start, size)]
        at = lax.broadcasted_iota(jnp.int32, rows.shape, 0)
        return jnp.sum(jnp.where(at == child, rows, 0), axis=0, keepdims=True)

    def row_spread(level, child):
        window = max(brows, 128)
        start = pl.multiple_of(p * brows // window * window, 128)
        row = map_of(level, child, start, window)
        picked = row[:, :brows]
        for t in range(1, window // brows):
            here = (p % (window // brows)) == t
            picked = jnp.where(here, row[:, t * brows : (t + 1) * brows], picked)
        r = picked - p * fronts
        target = jnp.where(r >= srows, r - srows, brows + r)
        at = lax.broadcasted_iota(jnp.int32, (fronts, brows), 0)
        return jnp.where(at == target, 1.0, 0.0).astype(BF16)

    def column_spread(level, child, q):
        start = pl.multiple_of(q * quarter, quarter)
        row = map_of(level, child, start, quarter)
        block = lax.broadcasted_iota(jnp.int32, (1, quarter), 1) // brows
        r = row - (q * (quarter // brows) + block) * fronts
        target = jnp.where(r >= srows, block * brows + r - srows, quarter + block * srows + r)
        at = lax.broadcasted_iota(jnp.int32, (quarter + qsep, quarter), 0)
        return jnp.where(at == target, 1.0, 0.0).astype(BF16)

    def place(block, rows, columns):
        high, low = split(block)
        lifted = nn(rows, high) + nn(rows, low)
        high, low = split(lifted)
        border, sep = columns[:quarter], columns[quarter:]
        spread = nt(high, border) + nt(low, border)
        coupling = nt(sep, high[:brows]) + nt(sep, low[:brows])
        return spread, coupling

    def share_rows(w):
        mine = w.at[p]
        near = send(mine, mine, {"panel": partner})
        far = [
            (other * CORES + core, send(mine, mine, {"panel": other * CORES + core}))
            for other in others
        ]
        return near, far

    def relay_rows(w, near, far):
        relays = []
        for d, (_, copy) in enumerate(far, 1):
            copy.wait_recv()
            slot = w.at[(y + chips - d) % chips * CORES + core]
            relays.append(send(slot, slot, {"panel": partner}))
        near.wait_recv()
        for relay in relays:
            relay.wait_recv()

    def coupled_rows(level, v):
        front = s // 2 ** (level + 1)
        gains = scale_ref[level, pl.ds(front, 1), :]
        rows = jnp.transpose(v[...].reshape(SEP, brows))
        return product(rows * gains, inverse_ref[level] * gains)

    child = s
    sibling = sub1
    rows_own, rows_far = row_spread(0, child), row_spread(0, sibling)

    def total(k):
        for copy in b_copies[k]:
            copy.wait_recv()
        value = own[k, y] + a_recv[k, y]
        for d in range(chips - 1):
            value = value + b_recv[k, d]
        return value

    c_copies = []
    for k in range(2):
        c_send[k] = total(k)
        c_copies.append(send(c_send.at[k], c_recv.at[k], {"sub": sub1}))
    for j in range(2):
        q = second + j
        spread_own, coupling_own = place(total(2 + j), rows_own, column_spread(0, child, q))
        c_copies[j].wait_recv()
        spread_far, coupling_far = place(c_recv[j], rows_far, column_spread(0, sibling, q))
        spread = spread_own + spread_far
        bb0[j] = spread[:brows]
        w0[p, j] = spread[brows:]
        v0[q] = coupling_own + coupling_far
    mine = v0.at[pl.ds(second, 2)]
    v_copy = send(mine, mine, {"sub": sub1})
    near, far = share_rows(w0)
    q = 2 * bit0 + bit1
    group = s // 8 * 8
    child1 = s // 2
    sibling1 = s // 4 * 2 + (1 - bit1)
    child2 = s // 4
    sibling2 = s // 8 * 2 + (1 - bit2)
    v_copy.wait_recv()
    coupled = coupled_rows(0, v0)
    relay_rows(w0, near, far)

    def updated(j):
        return bb0[j] - product(coupled, w0[:, j].reshape(SEP, quarter))

    d_send[...] = updated(1 - bit1)
    copy = send(d_send, d_recv, {"sub": sub2})
    schur = updated(bit1)
    for level, child, sibling, received, w, v in (
        (1, child1, sibling1, d_recv, w1, v1),
        (2, child2, sibling2, e_recv, w2, v2),
    ):
        spread_own, coupling_own = place(
            schur, row_spread(level, child), column_spread(level, child, q)
        )
        rows_far, columns_far = row_spread(level, sibling), column_spread(level, sibling, q)
        copy.wait_recv()
        spread_far, coupling_far = place(received[...], rows_far, columns_far)
        spread = spread_own + spread_far
        w[p] = spread[brows:]
        v[q] = coupling_own + coupling_far
        mine = v.at[q]
        v_copies = [send(mine, mine, {"sub": sub}) for sub in (sub1, sub2, sub3)]
        near, far = share_rows(w)
        for v_copy in v_copies:
            v_copy.wait_recv()
        coupled = coupled_rows(level, v)
        relay_rows(w, near, far)
        schur = spread[:brows] - product(coupled, w[...].reshape(SEP, quarter))
        if level == 1:
            e_send[...] = schur
            copy = send(e_send, e_recv, {"sub": sub4})
    fin[q] = schur
    mine = fin.at[q]
    near = send(mine, mine, {"sub": sub1})
    far = send(mine, mine, {"sub": sub2})
    half = brows // 2
    near.wait_recv()
    slot = fin.at[2 * (1 - bit0) + bit1, pl.ds(0, half)]
    upper = send(slot, slot, {"sub": sub2})
    far.wait_recv()
    slot = fin.at[2 * bit0 + 1 - bit1, pl.ds(half, half)]
    lower = send(slot, slot, {"sub": sub1})
    upper.wait_recv()
    lower.wait_recv()
    for t in range(QUARTERS):
        out_ref[0, :, pl.ds(t * quarter, quarter)] = fin[t]
    for copy in started:
        copy.wait_send()


def body(border_factor, tile_mask, front_maps, sep_inverse, sep_scale):
    panels = lax.axis_size("panel")
    chips = panels // CORES
    brows = BORDER // panels
    srows = SEP // panels
    quarter = BORDER // QUARTERS
    qsep = SEP // QUARTERS
    copies = 4 + 4 * (chips - 1) + 2 + 3 * (1 + 2 * (chips - 1)) + 1 + 6 + 2 + 4
    vmem = pl.BlockSpec(memory_space=pltpu.VMEM)
    block = pltpu.VMEM((brows, quarter), F32)
    return pl.pallas_call(
        functools.partial(kernel, panels),
        out_shape=jax.ShapeDtypeStruct((1, brows, BORDER), F32),
        in_specs=[pl.BlockSpec(memory_space=pltpu.SMEM), vmem, vmem, vmem, vmem],
        out_specs=vmem,
        scratch_shapes=[
            pltpu.VMEM((BORDER, border_factor.shape[2]), BF16),
            pltpu.VMEM((4, chips, brows, quarter), F32),
            pltpu.VMEM((4, chips, brows, quarter), F32),
            pltpu.VMEM((4, chips, brows, quarter), F32),
            pltpu.VMEM((4, chips - 1, brows, quarter), F32),
            pltpu.VMEM((4, chips - 1, brows, quarter), F32),
            pltpu.VMEM((2, brows, quarter), F32),
            pltpu.VMEM((2, brows, quarter), F32),
            pltpu.VMEM((panels, 2, srows, quarter), F32),
            pltpu.VMEM((panels, srows, quarter), F32),
            pltpu.VMEM((panels, srows, quarter), F32),
            pltpu.VMEM((QUARTERS, qsep, brows), F32),
            pltpu.VMEM((QUARTERS, qsep, brows), F32),
            pltpu.VMEM((QUARTERS, qsep, brows), F32),
            pltpu.VMEM((2, brows, quarter), F32),
            block,
            block,
            block,
            block,
            pltpu.VMEM((QUARTERS, brows, quarter), F32),
            pltpu.SemaphoreType.DMA((copies,)),
            pltpu.SemaphoreType.DMA((copies,)),
        ],
        compiler_params=pltpu.CompilerParams(
            collective_id=0, has_side_effects=True, vmem_limit_bytes=50 * 2**20
        ),
    )(tile_mask, border_factor, front_maps, sep_inverse, sep_scale)


def solution(mesh):
    return jax.shard_map(
        body,
        mesh=mesh,
        in_specs=(P("sub", None, "panel"), P("sub", None, "panel"), P(), P(), P()),
        out_specs=P("sub", "panel", None),
        check_vma=False,
    )
```

profile of v0, /device:TPU:0, one launch (start us, length us, event | category | flops | bytes accessed | tf_op | source)
XLA Modules:
  0.0 94.3 jit_solution(3808958436489005711)
XLA Ops:
  0.0 0.0 copy-start
  0.0 1.6 %copy-done = bf16[1,1024,1024]{2,1,0:T(8,128)(2,1)S(1)} copy-done((bf16[1,1024,1024]{2,1,0:T(8,128)(2,1)S(1)}, bf16[1,1024,1024]{2,1,0:T(8,128)(2,1)}, u32[]{:S(2)}) %copy-start) | copy-done | bytes 2097176
  1.6 0.0 copy-start.1
  1.6 1.1 %copy-done.1 = f32[3,256,256]{2,1,0:T(8,128)S(1)} copy-done((f32[3,256,256]{2,1,0:T(8,128)S(1)}, f32[3,256,256]{2,1,0:T(8,128)}, u32[]{:S(2)}) %copy-start.1) | copy-done | bytes 786456
  2.7 0.0 copy-start.2
  2.7 0.9 copy-done.2
  3.6 0.0 copy-start.3
  3.6 0.7 copy-done.3
  4.4 0.0 copy-start.4
  4.4 0.7 copy-done.4
  5.0 88.2 %shard_map.55 = f32[1,256,1024]{2,1,0:T(8,128)S(1)} custom-call(s32[1,8,8]{2,1,0:T(8,128)S(1)} %copy-done.4, bf16[1,1024,1024]{2,1,0:T(8,128)(2,1)S(1)} %copy-done, s32[3,8,1024]{2,1,0:T(8,128)S(1)} %copy-done.2, f32[3,256,256]{2,1,0:T(8,128)S(1)} %copy-done.1, f32[3,8,256]{2,1,0:T(8,128)S(1)} %copy-done.3), custom_call_target="tpu_custom_call" | custom-call | tf_op jit(solution)/shard_map/pallas_call | solution.py:305
  93.3 1.0 %copy.7 = f32[1,256,1024]{2,1,0:T(8,128)} copy(f32[1,256,1024]{2,1,0:T(8,128)S(1)} %shard_map.55) | data formatting | bytes 2097152
Async XLA Ops:
  0.0 1.6 %copy-start = (bf16[1,1024,1024]{2,1,0:T(8,128)(2,1)S(1)}, bf16[1,1024,1024]{2,1,0:T(8,128)(2,1)}, u32[]{:S(2)}) copy-start(bf16[1,1024,1024]{2,1,0:T(8,128)(2,1)} %factor_ref.1) | copy-start | bytes 6291460
  1.6 1.1 %copy-start.1 = (f32[3,256,256]{2,1,0:T(8,128)S(1)}, f32[3,256,256]{2,1,0:T(8,128)}, u32[]{:S(2)}) copy-start(f32[3,256,256]{2,1,0:T(8,128)} %inverse_ref.1) | copy-start | bytes 2359300
  2.7 0.9 copy-start.2
  3.6 0.7 copy-start.3
  4.4 0.7 copy-start.4
where the time goes:
time: 94.6 us; the launch traced here: 94.3 us
  Pallas kernels  88.2 us (93%)
  local copies, waits for them, and re-layouts  6.01 us (6%)
    pallas_call x1, Pallas kernels, body(): pl.pallas_call(functools.partial(kernel, panels), out_shape=jax.ShapeDtyp...  88.2 us
    unnamed x11, local copies, waits for them, and re-layouts  6.01 us

commit v1 on v0

--- a/solution.py
+++ b/solution.py
@@ -38,12 +38,18 @@
 
 def kernel(
     panels,
+    mask_hbm,
+    factor_hbm,
+    maps_hbm,
+    inverse_hbm,
+    scale_hbm,
+    out_ref,
     mask_ref,
     factor_ref,
     maps_ref,
     inverse_ref,
     scale_ref,
-    out_ref,
+    load_sem,
     masked,
     a_send,
     a_recv,
@@ -85,6 +91,19 @@
     partner = y * CORES + 1 - core
     others = [(y + d) % chips for d in range(1, chips)]
 
+    loads = [pltpu.make_async_copy(mask_hbm.at[0], mask_ref, load_sem.at[0])]
+    for i in range(QUARTERS):
+        rows = pl.ds(i * quarter, quarter)
+        loads.append(
+            pltpu.make_async_copy(factor_hbm.at[0, rows], factor_ref.at[rows], load_sem.at[1 + i])
+        )
+    for i, (src, dst) in enumerate(
+        ((maps_hbm, maps_ref), (inverse_hbm, inverse_ref), (scale_hbm, scale_ref))
+    ):
+        loads.append(pltpu.make_async_copy(src, dst, load_sem.at[1 + QUARTERS + i]))
+    for load in loads:
+        load.start()
+
     barrier = pltpu.get_barrier_semaphore()
     greeted = [{"panel": partner}] + [
         {"panel": other * CORES + core} for other in others
@@ -108,11 +127,14 @@
         started.append(copy)
         return copy
 
-    for i in range(mask_ref.shape[1]):
-        for j in range(mask_ref.shape[2]):
-            keep = jnp.full((TILE, TILE), mask_ref[0, i, j].astype(F32), F32).astype(BF16)
+    loads[0].wait()
+    for i in range(mask_ref.shape[0]):
+        if i % (quarter // TILE) == 0:
+            loads[1 + i // (quarter // TILE)].wait()
+        for j in range(mask_ref.shape[1]):
+            keep = jnp.full((TILE, TILE), mask_ref[i, j].astype(F32), F32).astype(BF16)
             rows, cols = pl.ds(i * TILE, TILE), pl.ds(j * TILE, TILE)
-            masked[rows, cols] = factor_ref[0, rows, cols] * keep
+            masked[rows, cols] = factor_ref[rows, cols] * keep
 
     def rows_of(chip, core_there):
         start = pl.multiple_of((chip * CORES + core_there) * brows, brows)
@@ -121,28 +143,41 @@
     first = 2 * (1 - bit0)
     second = 2 * bit0
     order = (first, first + 1, second, second + 1)
-    a_copies, b_copies = [], []
+    a_copies, b_copies, near_copies = [], [], []
+    near_chip = y
+
+    def columns_of(q):
+        return masked[pl.ds(pl.multiple_of(q * quarter, quarter), quarter), :]
 
     def forward(k):
-        a_copies[k].wait_recv()
         copies = []
         for d, other in enumerate(others):
+            a_copies[k][d].wait_recv()
             b_send[k, d] = own[k, other] + a_recv[k, other]
             copies.append(send(b_send.at[k, d], b_recv.at[k, d], {"panel": other * CORES + core}))
         b_copies.append(copies)
 
     for k, q in enumerate(order):
-        columns = masked[pl.ds(pl.multiple_of(q * quarter, quarter), quarter), :]
-        for chip in range(chips):
-            a_send[k, chip] = nt(rows_of(chip, 1 - core), columns)
-        if k == 0:
-            pl.semaphore_wait(barrier, len(greeted))
-        a_copies.append(send(a_send.at[k], a_recv.at[k], {"panel": partner}))
-        for chip in range(chips):
-            own[k, chip] = nt(rows_of(chip, core), columns)
+        copies = []
+        for other in others:
+            a_send[k, other] = nt(rows_of(other, 1 - core), columns_of(q))
+            if not started:
+                pl.semaphore_wait(barrier, len(greeted))
+            copies.append(send(a_send.at[k, other], a_recv.at[k, other], {"panel": partner}))
+        a_copies.append(copies)
+        for other in others:
+            own[k, other] = nt(rows_of(other, core), columns_of(q))
         if k:
             forward(k - 1)
     forward(len(order) - 1)
+    for k, q in enumerate(order):
+        a_send[k, near_chip] = nt(rows_of(near_chip, 1 - core), columns_of(q))
+        near_copies.append(
+            send(a_send.at[k, near_chip], a_recv.at[k, near_chip], {"panel": partner})
+        )
+        own[k, near_chip] = nt(rows_of(near_chip, core), columns_of(q))
+    for load in loads[1 + QUARTERS :]:
+        load.wait()
 
     def map_of(level, child, start, size):
         rows = maps_ref[level, :, pl.ds(start, size)]
@@ -210,6 +245,7 @@
     rows_own, rows_far = row_spread(0, child), row_spread(0, sibling)
 
     def total(k):
+        near_copies[k].wait_recv()
         for copy in b_copies[k]:
             copy.wait_recv()
         value = own[k, y] + a_recv[k, y]
@@ -299,15 +335,22 @@
     srows = SEP // panels
     quarter = BORDER // QUARTERS
     qsep = SEP // QUARTERS
-    copies = 4 + 4 * (chips - 1) + 2 + 3 * (1 + 2 * (chips - 1)) + 1 + 6 + 2 + 4
+    copies = 4 + 8 * (chips - 1) + 2 + 3 * (1 + 2 * (chips - 1)) + 1 + 6 + 2 + 4
     vmem = pl.BlockSpec(memory_space=pltpu.VMEM)
+    hbm = pl.BlockSpec(memory_space=pltpu.HBM)
     block = pltpu.VMEM((brows, quarter), F32)
     return pl.pallas_call(
         functools.partial(kernel, panels),
         out_shape=jax.ShapeDtypeStruct((1, brows, BORDER), F32),
-        in_specs=[pl.BlockSpec(memory_space=pltpu.SMEM), vmem, vmem, vmem, vmem],
+        in_specs=[hbm] * 5,
         out_specs=vmem,
         scratch_shapes=[
+            pltpu.SMEM(tile_mask.shape[1:], jnp.int32),
+            pltpu.VMEM(border_factor.shape[1:], BF16),
+            pltpu.VMEM(front_maps.shape, jnp.int32),
+            pltpu.VMEM(sep_inverse.shape, F32),
+            pltpu.VMEM(sep_scale.shape, F32),
+            pltpu.SemaphoreType.DMA((1 + QUARTERS + 3,)),
             pltpu.VMEM((BORDER, border_factor.shape[2]), BF16),
             pltpu.VMEM((4, chips, brows, quarter), F32),
             pltpu.VMEM((4, chips, brows, quarter), F32),

time: 94.6 us -> 94.2 us (level)
  no operation moved by 1% of the time
where the time goes in v1:
time: 94.2 us; the launch traced here: 93.8 us
  Pallas kernels  87.8 us (93%)
  local copies, waits for them, and re-layouts  6.01 us (6%)
    pallas_call x1, Pallas kernels, body(): pl.pallas_call(functools.partial(kernel, panels), out_shape=jax.ShapeDtyp...  87.8 us
    unnamed x11, local copies, waits for them, and re-layouts  6.01 us

profile of v1, /device:TPU:0, one launch (start us, length us, event | category | flops | bytes accessed | tf_op | source)
XLA Modules:
  0.0 93.8 jit_solution(16834154408448574095)
XLA Ops:
  0.0 0.0 copy-start
  0.0 1.6 %copy-done = bf16[1,1024,1024]{2,1,0:T(8,128)(2,1)S(1)} copy-done((bf16[1,1024,1024]{2,1,0:T(8,128)(2,1)S(1)}, bf16[1,1024,1024]{2,1,0:T(8,128)(2,1)}, u32[]{:S(2)}) %copy-start) | copy-done | bytes 2097176
  1.6 0.0 copy-start.1
  1.6 1.1 %copy-done.1 = f32[3,256,256]{2,1,0:T(8,128)S(1)} copy-done((f32[3,256,256]{2,1,0:T(8,128)S(1)}, f32[3,256,256]{2,1,0:T(8,128)}, u32[]{:S(2)}) %copy-start.1) | copy-done | bytes 786456
  2.7 0.0 copy-start.2
  2.7 0.9 copy-done.2
  3.6 0.0 copy-start.3
  3.6 0.7 copy-done.3
  4.4 0.0 copy-start.4
  4.4 0.7 copy-done.4
  5.0 87.8 %shard_map.55 = f32[1,256,1024]{2,1,0:T(8,128)S(1)} custom-call(s32[1,8,8]{2,1,0:T(8,128)S(1)} %copy-done.4, bf16[1,1024,1024]{2,1,0:T(8,128)(2,1)S(1)} %copy-done, s32[3,8,1024]{2,1,0:T(8,128)S(1)} %copy-done.2, f32[3,256,256]{2,1,0:T(8,128)S(1)} %copy-done.1, f32[3,8,256]{2,1,0:T(8,128)S(1)} %copy-done.3), custom_call_target="tpu_custom_call" | custom-call | tf_op jit(solution)/shard_map/pallas_call | solution.py:342
  92.9 1.0 %copy.7 = f32[1,256,1024]{2,1,0:T(8,128)} copy(f32[1,256,1024]{2,1,0:T(8,128)S(1)} %shard_map.55) | data formatting | bytes 2097152
Async XLA Ops:
  0.0 1.6 %copy-start = (bf16[1,1024,1024]{2,1,0:T(8,128)(2,1)S(1)}, bf16[1,1024,1024]{2,1,0:T(8,128)(2,1)}, u32[]{:S(2)}) copy-start(bf16[1,1024,1024]{2,1,0:T(8,128)(2,1)} %factor_hbm.1) | copy-start | bytes 6291460
  1.6 1.1 %copy-start.1 = (f32[3,256,256]{2,1,0:T(8,128)S(1)}, f32[3,256,256]{2,1,0:T(8,128)}, u32[]{:S(2)}) copy-start(f32[3,256,256]{2,1,0:T(8,128)} %inverse_hbm.1) | copy-start | bytes 2359300
  2.7 0.9 copy-start.2
  3.6 0.7 copy-start.3
  4.4 0.7 copy-start.4

commit v2 on v1

--- a/solution.py
+++ b/solution.py
@@ -50,6 +50,7 @@
     inverse_ref,
     scale_ref,
     load_sem,
+    store_sem,
     masked,
     a_send,
     a_recv,
@@ -215,8 +216,8 @@
         coupling = nt(sep, high[:brows]) + nt(sep, low[:brows])
         return spread, coupling
 
-    def share_rows(w):
-        mine = w.at[p]
+    def share_rows(w, *at):
+        mine = w.at[(p, *at)]
         near = send(mine, mine, {"panel": partner})
         far = [
             (other * CORES + core, send(mine, mine, {"panel": other * CORES + core}))
@@ -224,11 +225,11 @@
         ]
         return near, far
 
-    def relay_rows(w, near, far):
+    def relay_rows(w, near, far, *at):
         relays = []
         for d, (_, copy) in enumerate(far, 1):
             copy.wait_recv()
-            slot = w.at[(y + chips - d) % chips * CORES + core]
+            slot = w.at[((y + chips - d) % chips * CORES + core, *at)]
             relays.append(send(slot, slot, {"panel": partner}))
         near.wait_recv()
         for relay in relays:
@@ -257,6 +258,7 @@
     for k in range(2):
         c_send[k] = total(k)
         c_copies.append(send(c_send.at[k], c_recv.at[k], {"sub": sub1}))
+    v_shares, w_shares = [], []
     for j in range(2):
         q = second + j
         spread_own, coupling_own = place(total(2 + j), rows_own, column_spread(0, child, q))
@@ -266,18 +268,19 @@
         bb0[j] = spread[:brows]
         w0[p, j] = spread[brows:]
         v0[q] = coupling_own + coupling_far
-    mine = v0.at[pl.ds(second, 2)]
-    v_copy = send(mine, mine, {"sub": sub1})
-    near, far = share_rows(w0)
+        v_shares.append(send(v0.at[q], v0.at[q], {"sub": sub1}))
+        w_shares.append(share_rows(w0, j))
     q = 2 * bit0 + bit1
     group = s // 8 * 8
     child1 = s // 2
     sibling1 = s // 4 * 2 + (1 - bit1)
     child2 = s // 4
     sibling2 = s // 8 * 2 + (1 - bit2)
-    v_copy.wait_recv()
+    relay_rows(w0, *w_shares[0], 0)
+    for v_share in v_shares:
+        v_share.wait_recv()
     coupled = coupled_rows(0, v0)
-    relay_rows(w0, near, far)
+    relay_rows(w0, *w_shares[1], 1)
 
     def updated(j):
         return bb0[j] - product(coupled, w0[:, j].reshape(SEP, quarter))
@@ -299,7 +302,7 @@
         w[p] = spread[brows:]
         v[q] = coupling_own + coupling_far
         mine = v.at[q]
-        v_copies = [send(mine, mine, {"sub": sub}) for sub in (sub1, sub2, sub3)]
+        v_copies = [send(mine, mine, {"sub": sub}) for sub in (sub3, sub1, sub2)]
         near, far = share_rows(w)
         for v_copy in v_copies:
             v_copy.wait_recv()
@@ -310,20 +313,37 @@
             e_send[...] = schur
             copy = send(e_send, e_recv, {"sub": sub4})
     fin[q] = schur
-    mine = fin.at[q]
-    near = send(mine, mine, {"sub": sub1})
-    far = send(mine, mine, {"sub": sub2})
     half = brows // 2
-    near.wait_recv()
-    slot = fin.at[2 * (1 - bit0) + bit1, pl.ds(0, half)]
-    upper = send(slot, slot, {"sub": sub2})
-    far.wait_recv()
-    slot = fin.at[2 * bit0 + 1 - bit1, pl.ds(half, half)]
-    lower = send(slot, slot, {"sub": sub1})
+    quarter1, quarter2 = 2 * (1 - bit0) + bit1, 2 * bit0 + 1 - bit1
+    stores = []
+
+    def part(at, h):
+        return fin.at[at, pl.ds(h * half, half)]
+
+    def store(at):
+        columns = pl.ds(pl.multiple_of(at * quarter, quarter), quarter)
+        copy = pltpu.make_async_copy(
+            fin.at[at], out_ref.at[0, :, columns], store_sem.at[len(stores)]
+        )
+        copy.start()
+        stores.append(copy)
+
+    near = [send(part(q, h), part(q, h), {"sub": sub1}) for h in (0, 1)]
+    far = [send(part(q, h), part(q, h), {"sub": sub2}) for h in (1, 0)]
+    store(q)
+    near[0].wait_recv()
+    upper = send(part(quarter1, 0), part(quarter1, 0), {"sub": sub2})
+    far[0].wait_recv()
+    lower = send(part(quarter2, 1), part(quarter2, 1), {"sub": sub1})
+    near[1].wait_recv()
+    store(quarter1)
+    far[1].wait_recv()
+    store(quarter2)
     upper.wait_recv()
     lower.wait_recv()
-    for t in range(QUARTERS):
-        out_ref[0, :, pl.ds(t * quarter, quarter)] = fin[t]
+    store(2 * (1 - bit0) + 1 - bit1)
+    for copy in stores:
+        copy.wait()
     for copy in started:
         copy.wait_send()
 
@@ -335,15 +355,14 @@
     srows = SEP // panels
     quarter = BORDER // QUARTERS
     qsep = SEP // QUARTERS
-    copies = 4 + 8 * (chips - 1) + 2 + 3 * (1 + 2 * (chips - 1)) + 1 + 6 + 2 + 4
-    vmem = pl.BlockSpec(memory_space=pltpu.VMEM)
+    copies = 4 + 8 * (chips - 1) + 2 + 4 * (1 + 2 * (chips - 1)) + 2 + 6 + 2 + 6
     hbm = pl.BlockSpec(memory_space=pltpu.HBM)
     block = pltpu.VMEM((brows, quarter), F32)
     return pl.pallas_call(
         functools.partial(kernel, panels),
         out_shape=jax.ShapeDtypeStruct((1, brows, BORDER), F32),
         in_specs=[hbm] * 5,
-        out_specs=vmem,
+        out_specs=hbm,
         scratch_shapes=[
             pltpu.SMEM(tile_mask.shape[1:], jnp.int32),
             pltpu.VMEM(border_factor.shape[1:], BF16),
@@ -351,6 +370,7 @@
             pltpu.VMEM(sep_inverse.shape, F32),
             pltpu.VMEM(sep_scale.shape, F32),
             pltpu.SemaphoreType.DMA((1 + QUARTERS + 3,)),
+            pltpu.SemaphoreType.DMA((QUARTERS,)),
             pltpu.VMEM((BORDER, border_factor.shape[2]), BF16),
             pltpu.VMEM((4, chips, brows, quarter), F32),
             pltpu.VMEM((4, chips, brows, quarter), F32),
@@ -375,7 +395,7 @@
             pltpu.SemaphoreType.DMA((copies,)),
         ],
         compiler_params=pltpu.CompilerParams(
-            collective_id=0, has_side_effects=True, vmem_limit_bytes=50 * 2**20
+            collective_id=0, has_side_effects=True, vmem_limit_bytes=67043328
         ),
     )(tile_mask, border_factor, front_maps, sep_inverse, sep_scale)
 

time: 94.2 us -> 86.6 us (0.919)
  Pallas kernels: 87.8 us -> 84.1 us
  local copies, waits for them, and re-layouts: 6.01 us -> 2.31 us
    pallas_call x1, Pallas kernels: 87.8 us -> 84.1 us  [body(): pl.pallas_call(functools.partial(kernel, panels), out_shape=jax.ShapeDtyp...]
    unnamed x11 -> x1, local copies, waits for them, and re-layouts: 6.01 us -> 2.31 us
where the time goes in v2:
time: 86.6 us; the launch traced here: 86.4 us
  Pallas kernels  84.1 us (97%)
  local copies, waits for them, and re-layouts  2.31 us (3%)
    pallas_call x1, Pallas kernels, body(): pl.pallas_call(functools.partial(kernel, panels), out_shape=jax.ShapeDtyp...  84.1 us
    unnamed x1, local copies, waits for them, and re-layouts  2.31 us

profile of v2, /device:TPU:0, one launch (start us, length us, event | category | flops | bytes accessed | tf_op | source)
XLA Modules:
  0.0 86.4 jit_solution(16037281268740646673)
XLA Ops:
  0.0 84.1 %shard_map.55 = f32[1,256,1024]{2,1,0:T(8,128)} custom-call(s32[1,8,8]{2,1,0:T(8,128)} %mask_hbm.1, bf16[1,1024,1024]{2,1,0:T(8,128)(2,1)} %factor_hbm.1, s32[3,8,1024]{2,1,0:T(8,128)} %maps_hbm.1, f32[3,256,256]{2,1,0:T(8,128)} %inverse_hbm.1, f32[3,8,256]{2,1,0:T(8,128)} %scale_hbm.1), custom_call_target="tpu_custom_call" | custom-call | tf_op jit(solution)/shard_map/pallas_call | solution.py:361
  84.1 2.3 %copy.7 = f32[1,256,1024]{2,1,0:T(8,128)} copy(f32[1,256,1024]{2,1,0:T(8,128)} %shard_map.55) | data formatting | bytes 2097152

commit v3 on v2

--- a/solution.py
+++ b/solution.py
@@ -207,9 +207,16 @@
         at = lax.broadcasted_iota(jnp.int32, (quarter + qsep, quarter), 0)
         return jnp.where(at == target, 1.0, 0.0).astype(BF16)
 
+    half = brows // 2
+
+    def lift(block, rows):
+        high, low = split(block)
+        return nn(rows, high) + nn(rows, low)
+
     def place(block, rows, columns):
-        high, low = split(block)
-        lifted = nn(rows, high) + nn(rows, low)
+        return settle(lift(block, rows), columns)
+
+    def settle(lifted, columns):
         high, low = split(lifted)
         border, sep = columns[:quarter], columns[quarter:]
         spread = nt(high, border) + nt(low, border)
@@ -285,8 +292,14 @@
     def updated(j):
         return bb0[j] - product(coupled, w0[:, j].reshape(SEP, quarter))
 
+    def send_halves(src, dst, sub):
+        return [
+            send(src.at[pl.ds(h * half, half)], dst.at[pl.ds(h * half, half)], {"sub": sub})
+            for h in range(2)
+        ]
+
     d_send[...] = updated(1 - bit1)
-    copy = send(d_send, d_recv, {"sub": sub2})
+    copies = send_halves(d_send, d_recv, sub2)
     schur = updated(bit1)
     for level, child, sibling, received, w, v in (
         (1, child1, sibling1, d_recv, w1, v1),
@@ -296,8 +309,12 @@
             schur, row_spread(level, child), column_spread(level, child, q)
         )
         rows_far, columns_far = row_spread(level, sibling), column_spread(level, sibling, q)
-        copy.wait_recv()
-        spread_far, coupling_far = place(received[...], rows_far, columns_far)
+        lifted = jnp.zeros((fronts, quarter), F32)
+        for h, copy in enumerate(copies):
+            copy.wait_recv()
+            at = slice(h * half, (h + 1) * half)
+            lifted = lifted + lift(received[at], rows_far[:, at])
+        spread_far, coupling_far = settle(lifted, columns_far)
         spread = spread_own + spread_far
         w[p] = spread[brows:]
         v[q] = coupling_own + coupling_far
@@ -311,9 +328,8 @@
         schur = spread[:brows] - product(coupled, w[...].reshape(SEP, quarter))
         if level == 1:
             e_send[...] = schur
-            copy = send(e_send, e_recv, {"sub": sub4})
+            copies = send_halves(e_send, e_recv, sub4)
     fin[q] = schur
-    half = brows // 2
     quarter1, quarter2 = 2 * (1 - bit0) + bit1, 2 * bit0 + 1 - bit1
     stores = []
 
@@ -355,7 +371,7 @@
     srows = SEP // panels
     quarter = BORDER // QUARTERS
     qsep = SEP // QUARTERS
-    copies = 4 + 8 * (chips - 1) + 2 + 4 * (1 + 2 * (chips - 1)) + 2 + 6 + 2 + 6
+    copies = 4 + 8 * (chips - 1) + 2 + 4 * (1 + 2 * (chips - 1)) + 2 + 6 + 4 + 6
     hbm = pl.BlockSpec(memory_space=pltpu.HBM)
     block = pltpu.VMEM((brows, quarter), F32)
     return pl.pallas_call(

time: 86.6 us -> 86.5 us (level)
  no operation moved by 1% of the time
where the time goes in v3:
time: 86.5 us; the launch traced here: 86.4 us
  Pallas kernels  84.1 us (97%)
  local copies, waits for them, and re-layouts  2.31 us (3%)
    pallas_call x1, Pallas kernels, body(): pl.pallas_call(functools.partial(kernel, panels), out_shape=jax.ShapeDtyp...  84.1 us
    unnamed x1, local copies, waits for them, and re-layouts  2.31 us

profile of v3, /device:TPU:0, one launch (start us, length us, event | category | flops | bytes accessed | tf_op | source)
XLA Modules:
  0.0 86.4 jit_solution(10042024145436977999)
XLA Ops:
  0.0 84.1 %shard_map.55 = f32[1,256,1024]{2,1,0:T(8,128)} custom-call(s32[1,8,8]{2,1,0:T(8,128)} %mask_hbm.1, bf16[1,1024,1024]{2,1,0:T(8,128)(2,1)} %factor_hbm.1, s32[3,8,1024]{2,1,0:T(8,128)} %maps_hbm.1, f32[3,256,256]{2,1,0:T(8,128)} %inverse_hbm.1, f32[3,8,256]{2,1,0:T(8,128)} %scale_hbm.1), custom_call_target="tpu_custom_call" | custom-call | tf_op jit(solution)/shard_map/pallas_call | solution.py:377
  84.1 2.3 %copy.7 = f32[1,256,1024]{2,1,0:T(8,128)} copy(f32[1,256,1024]{2,1,0:T(8,128)} %shard_map.55) | data formatting | bytes 2097152

commit v4 on v3

--- a/solution.py
+++ b/solution.py
@@ -337,10 +337,7 @@
         return fin.at[at, pl.ds(h * half, half)]
 
     def store(at):
-        columns = pl.ds(pl.multiple_of(at * quarter, quarter), quarter)
-        copy = pltpu.make_async_copy(
-            fin.at[at], out_ref.at[0, :, columns], store_sem.at[len(stores)]
-        )
+        copy = pltpu.make_async_copy(fin.at[at], out_ref.at[at], store_sem.at[len(stores)])
         copy.start()
         stores.append(copy)
 
@@ -374,9 +371,9 @@
     copies = 4 + 8 * (chips - 1) + 2 + 4 * (1 + 2 * (chips - 1)) + 2 + 6 + 4 + 6
     hbm = pl.BlockSpec(memory_space=pltpu.HBM)
     block = pltpu.VMEM((brows, quarter), F32)
-    return pl.pallas_call(
+    quarters = pl.pallas_call(
         functools.partial(kernel, panels),
-        out_shape=jax.ShapeDtypeStruct((1, brows, BORDER), F32),
+        out_shape=jax.ShapeDtypeStruct((QUARTERS, brows, quarter), F32),
         in_specs=[hbm] * 5,
         out_specs=hbm,
         scratch_shapes=[
@@ -415,6 +412,19 @@
         ),
     )(tile_mask, border_factor, front_maps, sep_inverse, sep_scale)
 
+    def join(quarters_ref, out_ref):
+        for t in range(QUARTERS):
+            out_ref[0, :, t * quarter : (t + 1) * quarter] = quarters_ref[t]
+
+    steps = 2
+    return pl.pallas_call(
+        join,
+        grid=(steps,),
+        out_shape=jax.ShapeDtypeStruct((1, brows, BORDER), F32),
+        in_specs=[pl.BlockSpec((QUARTERS, brows // steps, quarter), lambda i: (0, i, 0))],
+        out_specs=pl.BlockSpec((1, brows // steps, BORDER), lambda i: (0, i, 0)),
+    )(quarters)
+
 
 def solution(mesh):
     return jax.shard_map(

time: 86.5 us -> 86.3 us (level)
  local copies, waits for them, and re-layouts: 2.31 us -> 0 us
  Pallas kernels: 84.1 us -> 86.1 us
    unnamed x1 -> x0, local copies, waits for them, and re-layouts: 2.31 us -> none
    pallas_call x0 -> x1, Pallas kernels: none -> 2.06 us  [body(): pl.pallas_call(join, grid=(steps,), out_shape=jax.ShapeDtypeStruct((1, br...]
where the time goes in v4:
time: 86.3 us; the launch traced here: 86.1 us
  Pallas kernels  86.1 us (100%)
    pallas_call x1, Pallas kernels, body(): pl.pallas_call(functools.partial(kernel, panels), out_shape=jax.ShapeDtyp...  84 us
    pallas_call x1, Pallas kernels, body(): pl.pallas_call(join, grid=(steps,), out_shape=jax.ShapeDtypeStruct((1, br...  2.06 us

profile of v4, /device:TPU:0, one launch (start us, length us, event | category | flops | bytes accessed | tf_op | source)
XLA Modules:
  0.0 86.1 jit_solution(15113729358992342498)
XLA Ops:
  0.0 84.0 %shard_map.55.quarters_ref = f32[4,256,256]{2,1,0:T(8,128)} custom-call(s32[1,8,8]{2,1,0:T(8,128)} %mask_hbm.1, bf16[1,1024,1024]{2,1,0:T(8,128)(2,1)} %factor_hbm.1, s32[3,8,1024]{2,1,0:T(8,128)} %maps_hbm.1, f32[3,256,256]{2,1,0:T(8,128)} %inverse_hbm.1, f32[3,8,256]{2,1,0:T(8,128)} %scale_hbm.1), custom_call_target="tpu_custom_call" | custom-call | tf_op jit(solution)/shard_map/pallas_call | solution.py:374
  84.0 2.1 %shard_map.56 = f32[1,256,1024]{2,1,0:T(8,128)} custom-call(f32[4,256,256]{2,1,0:T(8,128)} %shard_map.55.quarters_ref), custom_call_target="tpu_custom_call" | custom-call | tf_op jit(solution)/shard_map/pallas_call | solution.py:420
